TPU v7x, 512 devices: a whole 4x8x8 slice. The times are simulated.
512 devices in a mesh: ka: 32 (over x, z), ba: 16 (over y, core).
Axes of the slice: x: 4, y: 8, z: 8, core: 2. Of those that a mesh axis runs over, the one named last changes fastest.
Arguments:
- density: float32 [2, 8192, 4096], P(None, 'ka', 'ba'), may hold values from -6 to 6
- h_bands: float32 [2, 8192, 4096], P(None, ('ka', 'ba')), may hold values from -0.75 to 0.75
- coupling: bfloat16 [64, 4, 128, 128], P('ka'), may hold values from -0.03125 to 0.03125
- donors: int32 [64, 4], P('ka'), may hold values from 0 to 63, as said below
- counts: int32 [64], P('ka'), may hold values from 2 to 4, as said below
Outputs:
- evolved: float32 [2, 8192, 4096], P(None, 'ka', 'ba')
Inputs may be any that keep to these rules, and one draw needn't show every extreme that they name: donors[t] holds 4 different tiles, each within 2 tiles of t in the cyclic order of the 64 tiles; donors[t, 0] = t. `counts`: some tile uses all 4 slots.
All inputs are finite; a program needn't handle non-finite values.
Results may differ from a plain program's by a relative error of at most 0.0013.
Values may be sent and summed in bfloat16 or wider, within the bound.
A program may use at most 64 MiB of HBM per device.

v0:
```python
import jax
import jax.numpy as jnp
from jax import lax
from jax.experimental import pallas as pl
from jax.experimental.pallas import tpu as pltpu
from jax.sharding import PartitionSpec as P

NB = 64
TILE = 128
ND = 4
REACH = 2
TILES = 64
GROUP = 16
PART = 8
ROWS = 32
HALF = NB * PART
MESH = pl.DeviceIdType.MESH
F32, BF16, I16 = jnp.float32, jnp.bfloat16, jnp.int16
TOP = 32760.0

step_size = 0.25


def low_half(shape):
    return lax.broadcasted_iota(jnp.int32, shape, len(shape) - 1) < NB


def merge(real, imag):
    low = low_half(real.shape)
    first = jnp.where(low, real, pltpu.roll(imag, NB, 1))
    second = jnp.where(low, pltpu.roll(real, NB, 1), imag)
    return first, second


def split(first, second):
    low = low_half(first.shape)
    real = jnp.where(low, first, pltpu.roll(second, NB, 1))
    imag = jnp.where(low, pltpu.roll(first, NB, 1), second)
    return real, imag


def encode(*parts):
    top = parts[0][:1] * 0 + 1e-30
    for part in parts:
        top = jnp.maximum(top, jnp.max(jnp.abs(part), axis=0, keepdims=True))
    turn = TOP / top
    codes = [jnp.round(part * turn).astype(jnp.int32).astype(I16) for part in parts]
    return codes, top * (1.0 / TOP)


def decode(codes, scale):
    return codes.astype(jnp.int32).astype(F32) * scale


def halves(values):
    high = values.astype(BF16)
    return high, (values - high.astype(F32)).astype(BF16)


def rate(hamilton, state):
    sign = jnp.where(low_half(state.shape), 1.0, -1.0).astype(F32)
    turned_s = pltpu.roll(state, NB, 1) * sign
    turned_h = pltpu.roll(hamilton, NB, 1) * sign
    right_high, right_low = halves(
        jnp.concatenate([turned_s, state, turned_h, hamilton], axis=0)
    )
    left_high, left_low = halves(jnp.concatenate([hamilton, -state], axis=1))
    left = jnp.concatenate([left_high, left_low], axis=0)
    right = jnp.concatenate([right_high, right_low], axis=1)
    out = jnp.dot(left, right, preferred_element_type=F32)
    return out[:NB, :TILE] + (out[:NB, TILE:] + out[NB:, :TILE])


def kernel(
    dens_hbm, h_hbm, coup_hbm, donors_hbm, counts_hbm, out,
    dens, hraw, coup, donors, counts, low0, halo0, mix, hband, state, ham, change, sigma,
    whole_s, whole_r, enc_s, enc_r, scale_s, scale_r, mid_s, mid_r, halo1,
    load_sem, enc_ss, enc_rs, scale_ss, scale_rs, last_rs, last_scale_rs,
    mid_ss, mid_rs, halo0_ss, halo0_rs, halo1_ss, halo1_rs,
):
    me = lax.axis_index("ba")
    mine = lax.axis_index("ka")
    ring = lax.axis_size("ka")
    sides = (lax.rem(mine + 1, ring), lax.rem(mine + ring - 1, ring))

    pairs = (
        (dens_hbm, dens),
        (coup_hbm, coup),
        (h_hbm, hraw),
        (donors_hbm, donors),
        (counts_hbm, counts),
    )
    loads = [pltpu.make_async_copy(a, b, load_sem.at[i]) for i, (a, b) in enumerate(pairs)]
    for load in loads:
        load.start()

    barrier = pltpu.get_barrier_semaphore()
    for i in range(1, GROUP):
        pl.semaphore_signal(
            barrier, inc=1, device_id={"ba": lax.rem(me + i, GROUP)}, device_id_type=MESH
        )
    for side in sides:
        pl.semaphore_signal(barrier, inc=1, device_id={"ka": side}, device_id_type=MESH)

    def partner(i):
        step = (1 - 2 * lax.rem(i, 2)) * ((i + 1) // 2)
        return lax.rem(me + GROUP // 2 + step, GROUP)

    def to_ba(src, dst, send_sem, recv_sem, there):
        return pltpu.make_async_remote_copy(
            src_ref=src,
            dst_ref=dst,
            send_sem=send_sem,
            recv_sem=recv_sem,
            device_id={"ba": there},
            device_id_type=MESH,
        )

    def to_ka(src, dst, send_sem, recv_sem, side):
        return pltpu.make_async_remote_copy(
            src_ref=src,
            dst_ref=dst,
            send_sem=send_sem,
            recv_sem=recv_sem,
            device_id={"ka": sides[side]},
            device_id_type=MESH,
        )

    others = pl.ds(0, GROUP - 1)

    def codes_of(slot, sending, which):
        if slot == 0:
            return (whole_s if sending else whole_r).at[which]
        return (enc_s if sending else enc_r).at[slot - 1, which]

    def enc_copy(slot, there, group=None):
        return to_ba(
            codes_of(slot, True, there),
            codes_of(slot, False, me),
            enc_ss.at[slot],
            enc_rs.at[slot] if slot < 6 else last_rs.at[group],
            there,
        )

    def enc_all(slot, which=others, group=0):
        ref = codes_of(slot, False, which)
        recv_sem = enc_rs.at[slot] if slot < 6 else last_rs.at[group]
        return to_ba(ref, ref, enc_ss.at[slot], recv_sem, me)

    def scale_copy(slot, there, group=None):
        return to_ba(
            scale_s.at[slot, there],
            scale_r.at[slot, me],
            scale_ss.at[slot],
            scale_rs.at[slot] if slot < 6 else last_scale_rs.at[group],
            there,
        )

    def scale_all(slot, which=others, group=0):
        ref = scale_r.at[slot, which]
        recv_sem = scale_rs.at[slot] if slot < 6 else last_scale_rs.at[group]
        return to_ba(ref, ref, scale_ss.at[slot], recv_sem, me)

    def halo0_copy(side, chunk):
        cut = pl.ds(2 * chunk, 2)
        return to_ka(
            low0.at[cut],
            halo0.at[side, cut],
            halo0_ss.at[side, chunk],
            halo0_rs.at[side, chunk],
            side,
        )

    def mid_copy(chunk, there, group):
        return to_ba(
            mid_s.at[chunk, there],
            mid_r.at[chunk, me],
            mid_ss.at[chunk],
            mid_rs.at[chunk, group],
            there,
        )

    def mid_group(chunk, which, group):
        ref = mid_r.at[chunk, which]
        return to_ba(ref, ref, mid_ss.at[chunk], mid_rs.at[chunk, group], me)

    def halo1_copy(side, chunk, src):
        return to_ka(
            mid_r.at[chunk, src],
            halo1.at[side, chunk, src],
            halo1_ss.at[side, chunk],
            halo1_rs.at[side, chunk],
            side,
        )

    def halo1_all(side, chunk):
        ref = halo1.at[side, chunk]
        return to_ka(ref, ref, halo1_ss.at[side, chunk], halo1_rs.at[side, chunk], side)

    def momenta(block, half):
        return pl.ds(pl.multiple_of(block * GROUP + half * PART, PART), PART)

    def rows(half, block):
        return pl.ds(pl.multiple_of(half * HALF + block * ROWS, ROWS), ROWS)

    def parts_of(there):
        return [sigma[:, momenta(there, half), :].reshape(ROWS, TILE) for half in range(2)]

    def by_partner(put, start, near=False):
        def body(n, carry):
            order = [GROUP - 2 - 3 * n - i if near else 3 * n + i for i in range(3)]
            for i in order:
                put(i, partner(i))
            for i in order:
                start(i, partner(i))
            return carry

        lax.fori_loop(0, (GROUP - 1) // 3, body, 0)

    def send_codes(slot, put, group=False):
        def start(i, there):
            of = (i + 1) // 2 if group else None
            enc_copy(slot, there, of).start()
            scale_copy(slot, there, of).start()

        sending = whole_s if slot == 0 else enc_s
        by_partner(lambda i, there: put(sending, scale_s, there, there), start)
        put(whole_r if slot == 0 else enc_r, scale_r, me, me)

    loads[0].wait()
    for t in range(2):
        cut = pl.ds(t * TILE, TILE)
        for a, values in zip((2 * t, 2 * t + 1), merge(dens[0, :, cut], dens[1, :, cut])):
            low0[a] = values.astype(BF16)
            sigma[a] = values
        if t == 0:
            pl.semaphore_wait(barrier, GROUP + 1)
        for side in range(2):
            halo0_copy(side, t).start()

    def put_whole(codes_ref, scale_ref, slot, there):
        codes, scale = encode(*parts_of(there))
        for half in range(2):
            codes_ref[slot, pl.ds(half * ROWS, ROWS), :] = codes[half]
        scale_ref[0, slot] = scale

    send_codes(0, put_whole)

    for load in (loads[1], loads[3], loads[4]):
        load.wait()
    for t in range(2):
        tile = mine * 2 + t
        for position in range(2 + 2 * REACH):
            block = jnp.zeros((TILE, TILE), F32)
            if 0 <= position - t <= 2 * REACH:
                for s in range(ND):
                    offset = lax.rem(donors[t, s] - tile + REACH + TILES, TILES)
                    used = jnp.logical_and(offset == position - t, counts[t] > s)
                    weight = jnp.where(used, -1.0, 0.0).astype(F32)
                    block = block + coup[t, s].astype(F32) * weight
            mix[pl.ds(t * TILE, TILE), pl.ds(position * TILE, TILE)] = block.astype(BF16)

    def mixed(block, values):
        cut = pl.ds(block * 2 * TILE, 2 * TILE)
        return jnp.dot(mix[:, cut], values, preferred_element_type=F32)

    for a in range(4):
        sigma[a] = mixed(1, low0[a])

    loads[2].wait()

    def lay(step, carry):
        for i in range(4):
            t = step * 4 + i
            cut = pl.ds(pl.multiple_of(t * TILE, TILE), TILE)
            for half in range(2):
                part = pl.ds(half * PART, PART)
                first, second = merge(hraw[0, part, cut], hraw[1, part, cut])
                base = pl.multiple_of(half * HALF + t * 2 * PART, 2 * PART)
                hband[pl.ds(base, PART), :] = first
                hband[pl.ds(base + PART, PART), :] = second
        return carry

    lax.fori_loop(0, NB // 8, lay, 0)

    def send_bands(first_slot, chunk):
        slot, bands = first_slot + chunk, pl.ds(2 * chunk, 2)

        def put(codes_ref, scale_ref, index, there):
            parts = [
                sigma[bands, momenta(there, half), :].reshape(ROWS // 2, TILE) for half in range(2)
            ]
            codes, scale = encode(*parts)
            for half in range(2):
                codes_ref[slot - 1, index, pl.ds(half * ROWS // 2, ROWS // 2), :] = codes[half]
            scale_ref[slot, index] = scale

        send_codes(slot, put)

    def take_bands(first_slot, chunk):
        slot = first_slot + chunk
        scale_all(slot).wait_recv()
        enc_all(slot).wait_recv()

        def take(src, carry):
            values = decode(enc_r[slot - 1, src], scale_r[slot, src])
            for half in range(2):
                base = half * HALF + src * ROWS + chunk * ROWS // 2
                cut = pl.ds(pl.multiple_of(base, ROWS // 2), ROWS // 2)
                ham[cut, :] = hband[cut, :] + values[half * ROWS // 2 : (half + 1) * ROWS // 2]
            return carry

        lax.fori_loop(0, GROUP, take, 0)

    for chunk in range(2):
        for side in range(2):
            halo0_copy(side, chunk).wait_recv()
        for a in (2 * chunk, 2 * chunk + 1):
            sigma[a] += mixed(0, halo0[0, a]) + mixed(2, halo0[1, a])
        send_bands(1, chunk)

    scale_all(0).wait_recv()
    enc_all(0).wait_recv()

    def take_state(src, carry):
        values = decode(whole_r[src], scale_r[0, src])
        for half in range(2):
            state[rows(half, src), :] = values[half * ROWS : (half + 1) * ROWS]
        return carry

    lax.fori_loop(0, GROUP, take_state, 0)

    for chunk in range(2):
        take_bands(1, chunk)

    def each_momentum(half, use):
        def step(quad, carry):
            cuts = [pl.ds(half * HALF + quad * 4 + i, NB, stride=PART) for i in range(4)]
            states = [state[cut, :] for cut in cuts]
            rates = [rate(ham[cut, :], here) for cut, here in zip(cuts, states)]
            for cut, here, gained in zip(cuts, states, rates):
                use(cut, here, gained)
            return carry

        lax.fori_loop(0, 2, step, 0)

    def to_middle(cut, here, gained):
        state[cut, :] = here + (0.5 * step_size) * gained

    def to_change(cut, here, gained):
        change[cut, :] = step_size * gained

    for half in range(2):
        each_momentum(half, to_middle)

    def middle_of(chunk, there):
        parts = []
        for half in range(2):
            base = half * HALF + there * ROWS + chunk * ROWS // 2
            cut = pl.ds(pl.multiple_of(base, ROWS // 2), ROWS // 2)
            parts.append(state[cut, :].reshape(2, PART, TILE))
        return jnp.concatenate(parts, axis=1).astype(BF16)

    for chunk in range(2):

        def put_mid(i, there, chunk=chunk):
            mid_s[chunk, there] = middle_of(chunk, there)

        def start_mid(i, there, chunk=chunk):
            mid_copy(chunk, there, (i + 1) // 2).start()

        by_partner(put_mid, start_mid, near=True)
        mid_r[chunk, me] = middle_of(chunk, me)

    for chunk in range(2):
        for side in range(2):
            halo1_copy(side, chunk, me).start()

        def forward(group, members, chunk=chunk):
            mid_group(chunk, pl.ds(0, len(members)), group).wait_recv()
            for i in members:
                for side in range(2):
                    halo1_copy(side, chunk, partner(i)).start()

        def forward_pair(n, carry, forward=forward):
            group = GROUP // 2 - n
            forward(group, [2 * group, 2 * group - 1])
            return carry

        lax.fori_loop(1, GROUP // 2, forward_pair, 0)
        forward(0, [0])

    def band(ref, chunk, i):
        return ref[chunk, :, i].reshape(2 * TILE, TILE)

    for chunk in range(2):
        for i in range(2):
            sigma[2 * chunk + i] = mixed(1, band(mid_r, chunk, i))
    for chunk in range(2):
        for side in range(2):
            halo1_all(side, chunk).wait_recv()
        for i in range(2):
            left, right = (band(halo1.at[side], chunk, i) for side in range(2))
            sigma[2 * chunk + i] += mixed(0, left) + mixed(2, right)
        send_bands(3, chunk)

    for chunk in range(2):
        take_bands(3, chunk)

    for half in range(2):
        each_momentum(half, to_change)

        def put_change(codes_ref, scale_ref, index, there, half=half):
            (codes,), scale = encode(change[rows(half, there), :])
            codes_ref[4 + half, index] = codes
            scale_ref[5 + half, index] = scale

        send_codes(5 + half, put_change, group=True)

    for chunk in range(2):
        for side in range(2):
            halo0_copy(side, chunk).wait_send()
            halo1_all(side, chunk).wait_send()
        mid_group(chunk, others, 0).wait_send()
    for slot in range(5):
        enc_all(slot).wait_send()
        scale_all(slot).wait_send()

    def finish(half, sources):
        done = []
        for src in sources:
            gained = decode(enc_r[4 + half, src], scale_r[5 + half, src])
            part = momenta(src, half)
            for t in range(2):
                base = t * 2 * PART
                first, second = gained[base : base + PART], gained[base + PART : base + 2 * PART]
                cut = pl.ds(t * TILE, TILE)
                for c, change_c in enumerate(split(first, second)):
                    done.append((c, part, cut, dens[c, part, cut] + change_c))
        for c, part, cut, values in done:
            out[c, part, cut] = values

    scale_all(5).wait_recv()
    enc_all(5).wait_recv()

    def finish_first(step, carry):
        finish(0, [step * 4 + i for i in range(4)])
        return carry

    lax.fori_loop(0, GROUP // 4, finish_first, 0)
    finish(1, [me])

    def finish_group(group, members):
        which = pl.ds(0, len(members))
        enc_all(6, which, group).wait_recv()
        scale_all(6, which, group).wait_recv()
        finish(1, [partner(i) for i in members])

    finish_group(0, [0])

    def finish_pair(group, carry):
        finish_group(group, [2 * group - 1, 2 * group])
        return carry

    lax.fori_loop(1, GROUP // 2, finish_pair, 0)
    for slot in (5, 6):
        enc_all(slot).wait_send()
        scale_all(slot).wait_send()


def local(density, h_bands, coupling, donors, counts):
    whole = (GROUP, 2 * ROWS, TILE)
    codes = (6, GROUP, ROWS, TILE)
    scales = (7, GROUP, 1, TILE)
    middle = (2, GROUP, 2, GROUP, TILE)
    big = (NB * GROUP, TILE)
    dma = pltpu.SemaphoreType.DMA
    anywhere = pl.BlockSpec(memory_space=pl.ANY)
    operands = [
        pltpu.with_memory_space_constraint(x, pltpu.HBM)
        for x in (density, h_bands, coupling, donors, counts)
    ]
    return pl.pallas_call(
        kernel,
        out_shape=pltpu.VMEM(density.shape, F32),
        in_specs=[anywhere] * 5,
        out_specs=pl.BlockSpec(memory_space=pltpu.VMEM),
        scratch_shapes=[
            pltpu.VMEM(density.shape, F32),
            pltpu.VMEM(h_bands.shape, F32),
            pltpu.VMEM(coupling.shape, BF16),
            pltpu.SMEM(donors.shape, jnp.int32),
            pltpu.SMEM(counts.shape, jnp.int32),
            pltpu.VMEM((4, 2 * TILE, TILE), BF16),
            pltpu.VMEM((2, 4, 2 * TILE, TILE), BF16),
            pltpu.VMEM((2 * TILE, 6 * TILE), BF16),
            pltpu.VMEM(big, F32),
            pltpu.VMEM(big, F32),
            pltpu.VMEM(big, F32),
            pltpu.VMEM(big, F32),
            pltpu.VMEM((4, 2 * TILE, TILE), F32),
            pltpu.VMEM(whole, I16),
            pltpu.VMEM(whole, I16),
            pltpu.VMEM(codes, I16),
            pltpu.VMEM(codes, I16),
            pltpu.VMEM(scales, F32),
            pltpu.VMEM(scales, F32),
            pltpu.VMEM(middle, BF16),
            pltpu.VMEM(middle, BF16),
            pltpu.VMEM((2, *middle), BF16),
            dma((5,)),
            dma((7,)),
            dma((6,)),
            dma((7,)),
            dma((6,)),
            dma((GROUP // 2,)),
            dma((GROUP // 2,)),
            dma((2,)),
            dma((2, GROUP // 2)),
            dma((2, 2)),
            dma((2, 2)),
            dma((2, 2)),
            dma((2, 2)),
        ],
        compiler_params=pltpu.CompilerParams(
            collective_id=0, has_side_effects=True, vmem_limit_bytes=40 << 20
        ),
    )(*operands)


def solution(mesh):
    placed = (
        P(None, "ka", "ba"),
        P(None, ("ka", "ba"), None),
        P("ka", None, None, None),
        P("ka", None),
        P("ka"),
    )
    return jax.shard_map(
        local, mesh=mesh, in_specs=placed, out_specs=P(None, "ka", "ba"), check_vma=False
    )
```

profile of v0, /device:TPU:1, one launch (start us, length us, event | category | flops | bytes accessed | tf_op | source)
XLA Modules:
  0.0 63.5 jit_solution(6045312145495193216)
XLA Ops:
  0.0 62.7 %shard_map.55 = f32[2,256,256]{2,1,0:T(8,128)S(1)} custom-call(f32[2,256,256]{2,1,0:T(8,128)} %dens_hbm.1, f32[2,16,4096]{2,1,0:T(8,128)} %h_hbm.1, bf16[2,4,128,128]{3,2,1,0:T(8,128)(2,1)} %coup_hbm.1, s32[2,4]{1,0:T(2,128)} %donors_hbm.1, s32[2]{0:T(128)} %counts_hbm.1), custom_call_target="tpu_custom_call" | custom-call | tf_op jit(solution)/shard_map/pallas_call | solution.py:483
  62.7 0.8 %copy.7 = f32[2,256,256]{2,1,0:T(8,128)} copy(f32[2,256,256]{2,1,0:T(8,128)S(1)} %shard_map.55) | data formatting | bytes 1048576
where the time goes:
time: 63.7 us; the launch traced here: 63.5 us
  Pallas kernels  62.7 us (98%)
  local copies, waits for them, and re-layouts  0.8 us (1%)
    pallas_call x1, Pallas kernels, local(): pl.pallas_call(kernel, out_shape=pltpu.VMEM(density.shape, F32), in_specs...  62.7 us

commit v1 on v0

--- a/solution.py
+++ b/solution.py
@@ -128,24 +128,29 @@
 
     others = pl.ds(0, GROUP - 1)
 
-    def codes_of(slot, sending, which):
+    def codes_of(slot, sending, which, half):
         if slot == 0:
             return (whole_s if sending else whole_r).at[which]
-        return (enc_s if sending else enc_r).at[slot - 1, which]
-
-    def enc_copy(slot, there, group=None):
+        ref = enc_s if sending else enc_r
+        if half is None:
+            return ref.at[slot - 1, which]
+        return ref.at[slot - 1, which, pl.ds(half * ROWS // 2, ROWS // 2)]
+
+    def enc_sems(slot, half, group):
+        of = slot // 2 + 6 if half == 1 else slot
+        return enc_ss.at[of], last_rs.at[group] if slot == 6 else enc_rs.at[of]
+
+    def enc_copy(slot, there, group=None, half=None):
         return to_ba(
-            codes_of(slot, True, there),
-            codes_of(slot, False, me),
-            enc_ss.at[slot],
-            enc_rs.at[slot] if slot < 6 else last_rs.at[group],
+            codes_of(slot, True, there, half),
+            codes_of(slot, False, me, half),
+            *enc_sems(slot, half, group),
             there,
         )
 
-    def enc_all(slot, which=others, group=0):
-        ref = codes_of(slot, False, which)
-        recv_sem = enc_rs.at[slot] if slot < 6 else last_rs.at[group]
-        return to_ba(ref, ref, enc_ss.at[slot], recv_sem, me)
+    def enc_all(slot, which=others, group=0, half=None):
+        ref = codes_of(slot, False, which, half)
+        return to_ba(ref, ref, *enc_sems(slot, half, group), me)
 
     def scale_copy(slot, there, group=None):
         return to_ba(
@@ -217,14 +222,18 @@
 
         lax.fori_loop(0, (GROUP - 1) // 3, body, 0)
 
-    def send_codes(slot, put, group=False):
+    def send_codes(slot, put, group=False, halves_apart=False):
         def start(i, there):
             of = (i + 1) // 2 if group else None
-            enc_copy(slot, there, of).start()
+            enc_copy(slot, there, of, 0 if halves_apart else None).start()
             scale_copy(slot, there, of).start()
 
         sending = whole_s if slot == 0 else enc_s
         by_partner(lambda i, there: put(sending, scale_s, there, there), start)
+        if halves_apart:
+            by_partner(
+                lambda i, there: None, lambda i, there: enc_copy(slot, there, None, 1).start()
+            )
         put(whole_r if slot == 0 else enc_r, scale_r, me, me)
 
     loads[0].wait()
@@ -295,19 +304,21 @@
                 codes_ref[slot - 1, index, pl.ds(half * ROWS // 2, ROWS // 2), :] = codes[half]
             scale_ref[slot, index] = scale
 
-        send_codes(slot, put)
-
-    def take_bands(first_slot, chunk):
+        send_codes(slot, put, halves_apart=chunk == 1)
+
+    def take_bands(first_slot, chunk, half=None):
         slot = first_slot + chunk
-        scale_all(slot).wait_recv()
-        enc_all(slot).wait_recv()
+        if half != 1:
+            scale_all(slot).wait_recv()
+        enc_all(slot, half=half).wait_recv()
+        size = ROWS // 2
 
         def take(src, carry):
-            values = decode(enc_r[slot - 1, src], scale_r[slot, src])
-            for half in range(2):
-                base = half * HALF + src * ROWS + chunk * ROWS // 2
-                cut = pl.ds(pl.multiple_of(base, ROWS // 2), ROWS // 2)
-                ham[cut, :] = hband[cut, :] + values[half * ROWS // 2 : (half + 1) * ROWS // 2]
+            for h in range(2) if half is None else (half,):
+                part = enc_r[slot - 1, src, pl.ds(h * size, size), :]
+                base = h * HALF + src * ROWS + chunk * size
+                cut = pl.ds(pl.multiple_of(base, size), size)
+                ham[cut, :] = hband[cut, :] + decode(part, scale_r[slot, src])
             return carry
 
         lax.fori_loop(0, GROUP, take, 0)
@@ -330,8 +341,7 @@
 
     lax.fori_loop(0, GROUP, take_state, 0)
 
-    for chunk in range(2):
-        take_bands(1, chunk)
+    take_bands(1, 0)
 
     def each_momentum(half, use):
         def step(quad, carry):
@@ -351,6 +361,7 @@
         change[cut, :] = step_size * gained
 
     for half in range(2):
+        take_bands(1, 1, half)
         each_momentum(half, to_middle)
 
     def middle_of(chunk, there):
@@ -376,19 +387,20 @@
         for side in range(2):
             halo1_copy(side, chunk, me).start()
 
-        def forward(group, members, chunk=chunk):
-            mid_group(chunk, pl.ds(0, len(members)), group).wait_recv()
-            for i in members:
-                for side in range(2):
-                    halo1_copy(side, chunk, partner(i)).start()
-
-        def forward_pair(n, carry, forward=forward):
-            group = GROUP // 2 - n
-            forward(group, [2 * group, 2 * group - 1])
-            return carry
-
-        lax.fori_loop(1, GROUP // 2, forward_pair, 0)
-        forward(0, [0])
+    def forward(chunk, group):
+        members = [2 * group, 2 * group - 1] if group > 0 else [0]
+        mid_group(chunk, pl.ds(0, len(members)), group).wait_recv()
+        for i in members:
+            for side in range(2):
+                halo1_copy(side, chunk, partner(i)).start()
+
+    for group in (7, 6, 5):
+        forward(0, group)
+    for group in (4, 3, 2, 1, 0):
+        forward(0, group)
+        forward(1, group + 3)
+    for group in (2, 1, 0):
+        forward(1, group)
 
     def band(ref, chunk, i):
         return ref[chunk, :, i].reshape(2 * TILE, TILE)
@@ -404,10 +416,9 @@
             sigma[2 * chunk + i] += mixed(0, left) + mixed(2, right)
         send_bands(3, chunk)
 
-    for chunk in range(2):
-        take_bands(3, chunk)
-
+    take_bands(3, 0)
     for half in range(2):
+        take_bands(3, 1, half)
         each_momentum(half, to_change)
 
         def put_change(codes_ref, scale_ref, index, there, half=half):
@@ -423,7 +434,8 @@
             halo1_all(side, chunk).wait_send()
         mid_group(chunk, others, 0).wait_send()
     for slot in range(5):
-        enc_all(slot).wait_send()
+        for half in (0, 1) if slot in (2, 4) else (None,):
+            enc_all(slot, half=half).wait_send()
         scale_all(slot).wait_send()
 
     def finish(half, sources):
@@ -509,8 +521,8 @@
             pltpu.VMEM(middle, BF16),
             pltpu.VMEM((2, *middle), BF16),
             dma((5,)),
-            dma((7,)),
-            dma((6,)),
+            dma((9,)),
+            dma((9,)),
             dma((7,)),
             dma((6,)),
             dma((GROUP // 2,)),

time: 63.7 us -> 64.6 us (1.014)
  Pallas kernels: 62.7 us -> 63.7 us
    pallas_call x1, Pallas kernels: 62.7 us -> 63.7 us  [local(): pl.pallas_call(kernel, out_shape=pltpu.VMEM(density.shape, F32), in_specs...]
where the time goes in v1:
time: 64.6 us; the launch traced here: 64.5 us
  Pallas kernels  63.7 us (99%)
  local copies, waits for them, and re-layouts  0.8 us (1%)
    pallas_call x1, Pallas kernels, local(): pl.pallas_call(kernel, out_shape=pltpu.VMEM(density.shape, F32), in_specs...  63.7 us

profile of v1, /device:TPU:1, one launch (start us, length us, event | category | flops | bytes accessed | tf_op | source)
XLA Modules:
  0.0 64.5 jit_solution(9651958092754800020)
XLA Ops:
  0.0 63.7 %shard_map.55 = f32[2,256,256]{2,1,0:T(8,128)S(1)} custom-call(f32[2,256,256]{2,1,0:T(8,128)} %dens_hbm.1, f32[2,16,4096]{2,1,0:T(8,128)} %h_hbm.1, bf16[2,4,128,128]{3,2,1,0:T(8,128)(2,1)} %coup_hbm.1, s32[2,4]{1,0:T(2,128)} %donors_hbm.1, s32[2]{0:T(128)} %counts_hbm.1), custom_call_target="tpu_custom_call" | custom-call | tf_op jit(solution)/shard_map/pallas_call | solution.py:495
  63.7 0.8 %copy.7 = f32[2,256,256]{2,1,0:T(8,128)} copy(f32[2,256,256]{2,1,0:T(8,128)S(1)} %shard_map.55) | data formatting | bytes 1048576
